TPU v7x, 256 devices: a whole 4x4x8 slice. The times are simulated.
256 devices in a mesh: fsdp: 8 (over z_hi, y), tensor: 32 (over x, z_lo, core).
Axes of the slice: x: 4, y: 4, z: 8 (z_hi: 2, z_lo: 4; z = z_hi * 4 + z_lo), core: 2. Of those that a mesh axis runs over, the one named last changes fastest.
Arguments:
- momentum: bfloat16 [8192, 28672], P('fsdp', 'tensor'), may hold values from -6 to 6
- gradient: bfloat16 [8192, 28672], P('fsdp', 'tensor'), may hold values from -4 to 4
- factor: float32 [28672, 512], P('tensor', 'fsdp'), may hold values from -0.03125 to 0.03125
Outputs:
- new_momentum: bfloat16 [8192, 28672], P('fsdp', 'tensor')
- new_factor: float32 [28672, 512], P('tensor', 'fsdp')
- update: bfloat16 [8192, 28672], P('fsdp', 'tensor')
All inputs are finite; a program needn't handle non-finite values.
Results may differ from a plain program's by a relative error of at most 0.017.
Values may be sent and summed in bfloat16 or wider, within the bound.
No kernel may reach another device: no remote copies, remote signals or barrier semaphores. Data moves between devices by JAX's collectives and lax.ppermute only.
A program may use at most 64 MiB of HBM per device.

v0:
```python
import jax
import jax.numpy as jnp
from jax import lax
from jax.sharding import Mesh
from jax.sharding import PartitionSpec as P

D = 8192
FF = 28672
R = 512
TENSOR = ("tensor_0", "tensor_1", "tensor_2")


decay_rate = 0.95
epsilon = 1e-06


def from_everyone(value, axis):
    length = lax.axis_size(axis)
    return lax.all_to_all(
        jnp.broadcast_to(value[None], (length, *value.shape)), axis, 0, 0, tiled=True
    )


def laid_out(pieces, dim):
    lengths = list(pieces.shape[1:])
    lengths[dim] *= pieces.shape[0]
    return jnp.moveaxis(pieces, 0, dim).reshape(lengths)


def collect(value, axis, dim):
    pieces = from_everyone(value, axis)
    return laid_out(pieces, dim)


def padded_to(lines, length):
    spare = -lines.shape[0] % length
    if not spare:
        return lines
    return jnp.concatenate([lines, jnp.zeros((spare, *lines.shape[1:]), lines.dtype)])


def gather_axes(value, axes, dim):
    far, near = axes
    leading = from_everyone(value, far)
    pieces = jnp.swapaxes(from_everyone(leading, near), 0, 1)
    return laid_out(pieces.reshape(-1, *value.shape), dim)


def in_blocks(value, dim, length):
    before, after = (value.shape[:dim], value.shape[dim + 1 :])
    return jnp.moveaxis(value.reshape(*before, length, -1, *after), dim, 0)


def sum_at_owner(value, axis, dim):
    length = lax.axis_size(axis)
    pieces = lax.all_to_all(in_blocks(value, dim, length), axis, 0, 0, tiled=True)
    return jnp.sum(pieces, axis=0)


def sum_by_axis(value, axes, dim):
    far, near = axes
    pieces = in_blocks(value, dim, lax.axis_size(far))
    nearer = sum_at_owner(pieces, near, dim + 1)
    arrived = lax.all_to_all(nearer, far, split_axis=0, concat_axis=0, tiled=True)
    return arrived.sum(axis=0)


def sum_by_parts(value, axes):
    lines = value.reshape(-1, value.shape[-1])
    padded = padded_to(lines, lax.axis_size(axes[0]) * lax.axis_size(axes[1]))
    whole = gather_axes(sum_by_axis(padded, axes, 0), axes, 0)
    return lax.slice_in_dim(whole, 0, len(lines)).reshape(value.shape)


def over_copies(value, axis):
    everything = from_everyone(value, axis)
    return jnp.sum(everything, axis=0)


def on_device(momentum, gradient, factor):
    blended = (momentum.astype(jnp.float32) + gradient.astype(jnp.float32)).astype(jnp.bfloat16)
    lowered = factor.astype(jnp.bfloat16)
    columns = factor.shape[1]
    partial_left = jnp.dot(blended, collect(lowered, "fsdp", 1), preferred_element_type=jnp.float32)
    left_factor = sum_by_parts(partial_left, (("tensor_0", "tensor_1"), "tensor_2"))
    local_gram = lax.dot_general(
        left_factor, left_factor, (((0,), (0,)), ((), ())), precision=lax.Precision.HIGHEST
    )
    gram_matrix = lax.psum(local_gram, "fsdp")
    lower_factor = jnp.linalg.cholesky(gram_matrix)
    solved = jax.scipy.linalg.solve_triangular(lower_factor, left_factor.T, lower=True)
    orthonormal = solved.T.astype(jnp.bfloat16)
    partial_right = lax.dot_general(
        blended, orthonormal, (((0,), (0,)), ((), ())), preferred_element_type=jnp.float32
    )
    right_factor = lax.psum(partial_right.astype(jnp.bfloat16), "fsdp").astype(jnp.float32)
    square_sums = over_copies(jnp.sum(right_factor * right_factor, axis=0), TENSOR)
    inverse = lax.rsqrt(square_sums + epsilon)
    full_factor = right_factor * inverse[None, :]
    own_factor = lax.dynamic_slice_in_dim(full_factor, lax.axis_index("fsdp") * columns, columns, 1)
    product = lax.dot_general(
        orthonormal,
        right_factor.astype(jnp.bfloat16),
        (((1,), (1,)), ((), ())),
        preferred_element_type=jnp.float32,
    )
    stepped = lax.dot_general(
        orthonormal,
        full_factor.astype(jnp.bfloat16),
        (((1,), (1,)), ((), ())),
        preferred_element_type=jnp.float32,
    )
    new_momentum = (blended.astype(jnp.float32) - (1.0 - decay_rate) * product).astype(jnp.bfloat16)
    update = (stepped * jnp.sqrt(jnp.float32(D * FF / R))).astype(jnp.bfloat16)
    return (new_momentum, own_factor, update)


def solution(mesh):
    torus = Mesh(
        mesh.devices.reshape(mesh.shape["fsdp"], 4, 4, 2),
        ("fsdp", "tensor_0", "tensor_1", "tensor_2"),
    )
    return jax.shard_map(
        on_device,
        mesh=torus,
        in_specs=(P("fsdp", TENSOR), P("fsdp", TENSOR), P(TENSOR, "fsdp")),
        out_specs=(P("fsdp", TENSOR), P(TENSOR, "fsdp"), P("fsdp", TENSOR)),
        check_vma=False,
    )
```

profile of v0, /device:TPU:1, one launch (start us, length us, event | category | flops | bytes accessed | tf_op | source)
XLA Modules:
  0.0 529.2 jit_solution(15417045091283632723)
XLA Ops:
  7.2 1.1 convert_element_type.37
  8.3 1.0 broadcast_in_dim.9
  9.3 11.6 %all-to-all-start = ((bf16[8,896,64]{1,2,0:T(8,128)(2,1)}), bf16[8,896,64]{1,2,0:T(8,128)(2,1)S(1)}, u32[]{:S(2)}, u32[]{:S(2)}) async-start(bf16[8,896,64]{1,2,0:T(8,128)(2,1)} %broadcast_in_dim.9), calls=%async_computation | async-start | bytes 1835008 | tf_op jit(solution)/shard_map/all_to_all | solution.py:19
  21.0 3.2 add_convert_fusion
  24.2 13.0 %all-to-all-done = bf16[8,896,64]{1,2,0:T(8,128)(2,1)S(1)} async-done(((bf16[8,896,64]{1,2,0:T(8,128)(2,1)}), bf16[8,896,64]{1,2,0:T(8,128)(2,1)S(1)}, u32[]{:S(2)}, u32[]{:S(2)}) %all-to-all-start) | async-done | bytes 917536 | tf_op jit(solution)/shard_map/all_to_all | solution.py:19
  37.2 2.8 convolution_bitcast_fusion
  40.3 11.2 %all_to_all.31 = f32[2,16,32,512]{3,2,1,0:T(8,128)S(1)} all-to-all(f32[2,16,32,512]{3,2,1,0:T(8,128)S(1)} %copy.29), channel_id=1, replica_groups=mesh['fsdp'=8,'tensor_0'=4,'tensor_1'=4,'tensor_2'=2] {'tensor_2'}, dimensions={0} | all-to-all | bytes 4194304 | tf_op jit(solution)/shard_map/all_to_all | solution.py:56
  51.8 37.0 %all_to_all.32 = f32[16,32,512]{2,1,0:T(8,128)S(1)} all-to-all(f32[16,32,512]{2,1,0:T(8,128)S(1)} %reduce_sum.36), channel_id=1, replica_groups=mesh['fsdp'=8,'tensor_0'=4,'tensor_1'=4,'tensor_2'=2] {'tensor_0','tenso..., dimensions={0} | all-to-all | bytes 2097152 | tf_op jit(solution)/shard_map/all_to_all | solution.py:64
  88.9 30.9 %all_to_all.33 = f32[16,32,512]{2,1,0:T(8,128)S(1)} all-to-all(f32[16,32,512]{2,1,0:T(8,128)S(1)} %broadcast_in_dim.10), channel_id=1, replica_groups=mesh['fsdp'=8,'tensor_0'=4,'tensor_1'=4,'tensor_2'=2] {'tensor_0','tenso..., dimensions={0} | all-to-all | bytes 2097152 | tf_op jit(solution)/shard_map/all_to_all | solution.py:19
  120.1 6.8 %all_to_all.34 = f32[2,16,32,512]{3,2,1,0:T(8,128)S(1)} all-to-all(f32[2,16,32,512]{3,2,1,0:T(8,128)S(1)} %broadcast_in_dim.11), channel_id=1, replica_groups=mesh['fsdp'=8,'tensor_0'=4,'tensor_1'=4,'tensor_2'=2] {'tensor_2'}, dimensions={0} | all-to-all | bytes 4194304 | tf_op jit(solution)/shard_map/all_to_all | solution.py:19
  126.8 4.5 fusion.9
  131.4 1.6 copy.30
  133.0 2.1 copy.33
  135.1 97.7 %all-reduce.4.cloned.1.call-done = f32[512,512]{0,1:T(8,128)} async-done(((f32[512,512]{0,1:T(8,128)}), f32[512,512]{0,1:T(8,128)}) %all-reduce.4.cloned.1.call-update) | async-done | bytes 1048592 | tf_op jit(solution)/shard_map/psum | solution.py:89
  232.9 2.6 copy.32
  235.5 1.4 fusion.18
  237.0 1.0 copy-done.2
  237.9 11.7 %cholesky.104 = f32[128,128]{1,0:T(8,128)S(1)} custom-call(f32[128,128]{1,0:T(8,128)S(1)} %cholesky.266), custom_call_target="Cholesky" | custom-call | tf_op jit(solution)/shard_map/jit(cholesky)/cholesky | solution.py:90
  249.8 9.8 %custom-call.31 = f32[1,128,128]{1,2,0:T(8,128)S(1)} custom-call(f32[1,128,128]{2,1,0:T(8,128)S(1)} %get-tuple-element.45), custom_call_target="InvertDiagBlocksLowerTriangular" | custom-call | tf_op jit(solution)/shard_map/jit(cholesky)/cholesky | solution.py:90
  259.6 1.2 constant_dynamic-update-slice_fusion.3
  260.9 1.3 convolution_subtract_fusion.2
  262.1 11.7 %cholesky.217 = f32[128,128]{1,0:T(8,128)S(1)} custom-call(f32[128,128]{1,0:T(8,128)S(1)} %cholesky.270), custom_call_target="Cholesky" | custom-call | tf_op jit(solution)/shard_map/jit(cholesky)/cholesky | solution.py:90
  273.9 10.0 %custom-call.32 = f32[1,128,128]{1,2,0:T(8,128)S(1)} custom-call(f32[1,128,128]{2,1,0:T(8,128)S(1)} %get-tuple-element.42), custom_call_target="InvertDiagBlocksLowerTriangular" | custom-call | tf_op jit(solution)/shard_map/jit(cholesky)/cholesky | solution.py:90
  284.2 1.3 convolution_subtract_fusion.3
  285.5 11.7 %cholesky.238 = f32[128,128]{1,0:T(8,128)S(1)} custom-call(f32[128,128]{1,0:T(8,128)S(1)} %cholesky.275), custom_call_target="Cholesky" | custom-call | tf_op jit(solution)/shard_map/jit(cholesky)/cholesky | solution.py:90
  297.2 0.7 compare_reduce_fusion.1
  297.9 9.8 %custom-call.33 = f32[1,128,128]{1,2,0:T(8,128)S(1)} custom-call(f32[1,128,128]{2,1,0:T(8,128)S(1)} %get-tuple-element.39), custom_call_target="InvertDiagBlocksLowerTriangular" | custom-call | tf_op jit(solution)/shard_map/jit(cholesky)/cholesky | solution.py:90
  308.0 1.2 convolution_subtract_fusion.4
  309.2 11.7 %cholesky.255 = f32[128,128]{1,0:T(8,128)S(1)} custom-call(f32[128,128]{1,0:T(8,128)S(1)} %convolution_subtract_fusion.4), custom_call_target="Cholesky" | custom-call | tf_op jit(solution)/shard_map/jit(cholesky)/cholesky | solution.py:90
  324.8 1.5 select_select_fusion
  326.3 14.1 %while.1 = (s32[]{:T(128)}, f32[512,512]{1,0:T(8,128)}, s32[4,2]{0,1:T(2,128)S(1)}, f32[4,128,128]{2,1,0:T(8,128)}, s32[]{:T(128)}) while((s32[]{:T(128)}, f32[512,512]{1,0:T(8,128)}, s32[4,2]{0,1:T(2,128)S(1)}, f32[4,128,128]{2,1,0:T(8,128)}, s32[]{:T(128)}) %tuple.39), condition=%wide.while_cond, body=%wide.while_body.sunk | while | flops 2 | bytes 132705 | solution.py:91
  326.9 2.9 bitcast_dynamic-update-slice_fusion.2
  330.5 2.9 bitcast_dynamic-update-slice_fusion.2
  334.0 2.9 bitcast_dynamic-update-slice_fusion.2
  337.6 2.8 bitcast_dynamic-update-slice_fusion.2
  340.4 40.1 %custom-call.34 = f32[4,128,128]{1,2,0:T(8,128)S(1)} custom-call(f32[4,128,128]{2,1,0:T(8,128)} %get-tuple-element.10), custom_call_target="InvertDiagBlocksLowerTriangular" | custom-call | tf_op jit(solution)/shard_map/jit(_solve_triangular)/triangular_solve | solution.py:91
  381.1 1.4 convolution_subtract_fusion.1
  383.2 1.7 convolution_subtract_fusion
  385.6 2.2 fusion.12
  388.5 2.1 convolution_convert_fusion
  390.6 106.7 %all-reduce.6.cloned.1.call-done = bf16[896,512]{1,0:T(8,128)(2,1)} async-done(((bf16[896,512]{1,0:T(8,128)(2,1)}), bf16[896,512]{1,0:T(8,128)(2,1)}) %all-reduce.6.cloned.1.call-update) | async-done | bytes 917520 | tf_op jit(solution)/shard_map/psum | solution.py:96
  497.3 1.4 fusion.2
  498.8 0.7 broadcast_in_dim.12
  499.4 11.0 %all-to-all-start.5 = ((f32[32,1,512]{2,1,0:T(1,128)}), f32[32,1,512]{2,1,0:T(1,128)S(1)}, u32[]{:S(2)}, u32[]{:S(2)}) async-start(f32[32,1,512]{2,1,0:T(1,128)} %broadcast_in_dim.12), calls=%async_computation.5 | async-start | bytes 131072 | tf_op jit(solution)/shard_map/all_to_all | solution.py:19
  510.5 4.0 subtract_convert_fusion
  514.4 3.8 all-to-all-done.5
  518.8 0.9 copy.35
  519.7 2.5 multiply_convert_fusion
  (59 shorter events, 8.9 us)
Async XLA Ops:
  7.2 13.8 %copy-start.3 = (bf16[1024,896]{1,0:T(8,128)(2,1)S(1)}, bf16[1024,896]{1,0:T(8,128)(2,1)}, u32[]{:S(2)}) copy-start(bf16[1024,896]{1,0:T(8,128)(2,1)} %param.4) | copy-start | bytes 5505028
  9.3 27.9 %all-to-all-start = ((bf16[8,896,64]{1,2,0:T(8,128)(2,1)}), bf16[8,896,64]{1,2,0:T(8,128)(2,1)S(1)}, u32[]{:S(2)}, u32[]{:S(2)}) async-start(bf16[8,896,64]{1,2,0:T(8,128)(2,1)} %broadcast_in_dim.9), calls=%async_computation | async-start | bytes 1835008 | tf_op jit(solution)/shard_map/all_to_all | solution.py:19
  21.0 211.9 %all-reduce.4.cloned.1.call-start = ((), (), s32[]{:S(2)}) async-start(), calls=%async_computation.6 | async-start | bytes 2097152 | tf_op jit(solution)/shard_map/psum | solution.py:89
  131.4 365.9 %all-reduce.6.cloned.1.call-start = ((), (), s32[]{:S(2)}) async-start(), calls=%async_computation.7 | async-start | bytes 1835008 | tf_op jit(solution)/shard_map/psum | solution.py:96
  232.9 2.6 copy-start
  236.9 1.0 copy-start.2
  383.2 5.2 copy-start.6
  385.6 2.8 copy-start.8
  385.6 2.8 copy-start.4
  388.4 122.0 %copy-start.5 = (bf16[1024,896]{1,0:T(8,128)(2,1)S(1)}, bf16[1024,896]{1,0:T(8,128)(2,1)}, u32[]{:S(2)}) copy-start(bf16[1024,896]{1,0:T(8,128)(2,1)} %add_convert_fusion) | copy-start | bytes 5505028
  499.4 18.8 %all-to-all-start.5 = ((f32[32,1,512]{2,1,0:T(1,128)}), f32[32,1,512]{2,1,0:T(1,128)S(1)}, u32[]{:S(2)}, u32[]{:S(2)}) async-start(f32[32,1,512]{2,1,0:T(1,128)} %broadcast_in_dim.12), calls=%async_computation.5 | async-start | bytes 131072 | tf_op jit(solution)/shard_map/all_to_all | solution.py:19
  510.5 7.9 %copy-start.1 = (bf16[896,512]{1,0:T(8,128)(2,1)S(1)}, bf16[896,512]{1,0:T(8,128)(2,1)}, u32[]{:S(2)}) copy-start(bf16[896,512]{1,0:T(8,128)(2,1)} %all-reduce.6.cloned.1.call-done) | copy-start | bytes 2752516
  518.3 1.3 copy-start.7
  518.3 1.3 copy-start.9
Sparse Core Ops, SparseCore 0:
  131.5 101.3 all-reduce.3
  390.7 106.5 all-reduce.5
where the time goes:
time: 536 us; the launch traced here: 529 us
  waiting for transfers between devices  221 us (41%)
  other arithmetic  128 us (24%)
  blocking collectives  85.8 us (16%)
  matrix products  29.2 us (5%)
  local copies, waits for them, and re-layouts  25 us (5%)
  starting transfers between devices  22.7 us (4%)
  between operations  17.1 us (3%)
    psum x1, waiting for transfers between devices, on_device(): lax.psum(partial_right.astype(jnp.bfloat16), 'fsdp').astype(jnp.float32)  107 us
    psum x1, waiting for transfers between devices, on_device(): gram_matrix = lax.psum(local_gram, 'fsdp')  97.7 us
    another operation x14, other arithmetic, on_device(): lower_factor = jnp.linalg.cholesky(gram_matrix)  78.6 us
    another operation x3, other arithmetic, on_device(): jax.scipy.linalg.solve_triangular(lower_factor, left_factor.T, lower=True)  41.6 us
    all_to_all x2, blocking collectives, from_everyone(): lax.all_to_all(jnp.broadcast_to(value[None], (length, *value.shape)), axi...  37.6 us
    all_to_all x1, blocking collectives, sum_by_axis(): lax.all_to_all(nearer, far, split_axis=0, concat_axis=0, tiled=True)  37 us
    all_to_all x2, starting transfers between devices, from_everyone(): lax.all_to_all(jnp.broadcast_to(value[None], (length, *value.shape)), axi...  22.7 us
    all_to_all x2, waiting for transfers between devices, from_everyone(): lax.all_to_all(jnp.broadcast_to(value[None], (length, *value.shape)), axi...  16.8 us
  transfers between devices with their start and end apart: 4, of which 4 were waited for; matrix products, arithmetic and copies ran while one was open for 2% of the time, Pallas kernels for 0%

commit v1 on v0

v1 whole, which is shorter than its diff:
```python
import jax
import jax.numpy as jnp
from jax import lax
from jax.experimental import pallas as pl
from jax.experimental.pallas import tpu as pltpu
from jax.sharding import Mesh
from jax.sharding import PartitionSpec as P

D = 8192
FF = 28672
R = 512
FAR = 16
BLOCK = 128
BLOCKS = R // BLOCK
PAIRS = [(i, j) for i in range(BLOCKS) for j in range(i + 1)]
SUB = 8
TENSOR = ("far", "core")

decay_rate = 0.95
epsilon = 1e-06
f32 = jnp.float32
bf16 = jnp.bfloat16


def product(left, right, left_dim, right_dim, precision=None):
    return lax.dot_general(
        left, right, (((left_dim,), (right_dim,)), ((), ())), precision=precision, preferred_element_type=f32
    )


def exact(left, right, left_dim, right_dim):
    return product(left, right, left_dim, right_dim, lax.Precision.HIGHEST)


def added(terms):
    while len(terms) > 1:
        terms = [
            terms[i] + terms[i + 1] if i + 1 < len(terms) else terms[i] for i in range(0, len(terms), 2)
        ]
    return terms[0]


def spread(value):
    return jnp.broadcast_to(value, (SUB, BLOCK))


def small_inverse(entries):
    rest = [row[:] for row in entries]
    inverse = [None] * SUB
    upper = [[None] * SUB for _ in range(SUB)]
    for j in range(SUB):
        inverse[j] = lax.rsqrt(rest[j][j])
        for k in range(j + 1, SUB):
            upper[j][k] = rest[j][k] * inverse[j]
        for i in range(j + 1, SUB):
            for k in range(i, SUB):
                rest[i][k] = rest[i][k] - upper[j][i] * upper[j][k]
    result = [[None] * SUB for _ in range(SUB)]
    for j in range(SUB):
        result[j][j] = inverse[j]
        for i in range(j + 1, SUB):
            total = upper[j][i] * result[j][j]
            for k in range(j + 1, i):
                total = total + upper[k][i] * result[k][j]
            result[i][j] = -(inverse[i] * total)
    return result


def factor_block(held):
    sub = lax.broadcasted_iota(jnp.int32, (SUB, BLOCK), 0)
    rows = held[0:SUB, :]
    for panel in range(BLOCK // SUB):
        lo = panel * SUB
        left, right = rows[:, :BLOCK], rows[:, BLOCK:]
        entries = [[None] * SUB for _ in range(SUB)]
        for i in range(SUB):
            for k in range(i, SUB):
                entries[i][k] = spread(left[i : i + 1, lo + k : lo + k + 1])
        inverse = small_inverse(entries)
        columns = []
        for k in range(SUB):
            column = jnp.zeros((SUB, BLOCK), f32)
            for i in range(k, SUB):
                column = jnp.where(sub == i, inverse[i][k], column)
            columns.append(column)
        left = added([columns[k] * spread(left[k : k + 1, :]) for k in range(SUB)])
        right = added([columns[k] * spread(right[k : k + 1, :]) for k in range(SUB)])
        held[lo : lo + SUB, :BLOCK] = left
        held[lo : lo + SUB, BLOCK:] = right
        both = jnp.concatenate([left, right], axis=1)
        if lo + SUB < BLOCK:
            following = held[lo + SUB : lo + 2 * SUB, :]
            across = [spread(following[:, lo + k : lo + k + 1]) for k in range(SUB)]
            weights = [added([across[k] * inverse[i][k] for k in range(i + 1)]) for i in range(SUB)]
            next_left = following[:, :BLOCK] - added([weights[i] * spread(left[i : i + 1, :]) for i in range(SUB)])
            next_right = following[:, BLOCK:] - added([weights[i] * spread(right[i : i + 1, :]) for i in range(SUB)])
            rows = jnp.concatenate([next_left, next_right], axis=1)
        if lo + 2 * SUB < BLOCK:
            change = exact(left, both, 0, 0)
            held[lo + 2 * SUB :, :] = held[lo + 2 * SUB :, :] - change[lo + 2 * SUB :, :]


def inverse_kernel(gram_ref, high_ref, low_ref, gram, inverse, held):
    place = {pair: n for n, pair in enumerate(PAIRS)}
    gram[...] = gram_ref[...]
    inverse[...] = jnp.zeros((R, R), f32)
    row = lax.broadcasted_iota(jnp.int32, (BLOCK, BLOCK), 0)
    column = lax.broadcasted_iota(jnp.int32, (BLOCK, BLOCK), 1)
    identity = jnp.where(row == column, 1.0, 0.0).astype(f32)
    for b in range(BLOCKS):
        lo, hi = b * BLOCK, (b + 1) * BLOCK
        held[:, :BLOCK] = gram[place[b, b]]
        held[:, BLOCK:] = identity
        factor_block(held)
        own = held[:, BLOCK:]
        if b:
            inverse[lo:hi, :lo] = exact(own, inverse[lo:hi, :lo], 1, 0)
        inverse[lo:hi, lo:hi] = own
        lower = {i: exact(gram[place[i, b]], own, 1, 1) for i in range(b + 1, BLOCKS)}
        for i in range(b + 1, BLOCKS):
            for j in range(b + 1, i + 1):
                gram[place[i, j]] = gram[place[i, j]] - exact(lower[i], lower[j], 1, 1)
            into = slice(i * BLOCK, (i + 1) * BLOCK)
            inverse[into, :hi] = inverse[into, :hi] - exact(lower[i], inverse[lo:hi, :hi], 1, 0)
    high = inverse[...].astype(bf16)
    high_ref[...] = high
    low_ref[...] = (inverse[...] - high.astype(f32)).astype(bf16)


def inverse_factor(packed):
    whole = pl.BlockSpec(memory_space=pltpu.VMEM)
    return pl.pallas_call(
        inverse_kernel,
        out_shape=[jax.ShapeDtypeStruct((R, R), bf16)] * 2,
        in_specs=[whole],
        out_specs=[whole] * 2,
        scratch_shapes=[
            pltpu.VMEM((len(PAIRS), BLOCK, BLOCK), f32),
            pltpu.VMEM((R, R), f32),
            pltpu.VMEM((BLOCK, 2 * BLOCK), f32),
        ],
        compiler_params=pltpu.CompilerParams(vmem_limit_bytes=32 << 20),
        cost_estimate=pl.CostEstimate(flops=2 * R**3, bytes_accessed=2 << 20, transcendentals=R),
    )(packed)


def from_everyone(value, axis):
    length = lax.axis_size(axis)
    return lax.all_to_all(jnp.broadcast_to(value[None], (length, *value.shape)), axis, 0, 0, tiled=True)


def swapped(value):
    return lax.ppermute(value, "core", [(0, 1), (1, 0)])


def in_order(own, other, core):
    first = jnp.where(core == 0, own, other)
    second = jnp.where(core == 0, other, own)
    return jnp.concatenate([first, second])


def on_device(momentum, gradient, factor):
    core, far, row_group = lax.axis_index("core"), lax.axis_index("far"), lax.axis_index("fsdp")
    columns = factor.shape[1]
    lowered = factor.T.astype(bf16)
    all_lowered = from_everyone(lowered, "fsdp").reshape(R, -1)
    blended = (momentum.astype(f32) + gradient.astype(f32)).astype(bf16)
    half = blended.shape[0] // 2
    own_rows = lax.dynamic_slice_in_dim(blended, core * half, half, 0)
    other_rows = lax.dynamic_slice_in_dim(blended, (1 - core) * half, half, 0)

    sent = product(other_rows, all_lowered, 1, 1).astype(bf16)
    arrived = swapped(sent)
    partial_left = (product(own_rows, all_lowered, 1, 1) + arrived.astype(f32)).astype(bf16)
    pieces = lax.all_to_all(partial_left.reshape(FAR, -1, R), "far", 0, 0, tiled=True)
    left_rows = jnp.sum(pieces.astype(f32), axis=0).astype(bf16)
    own_left = from_everyone(left_rows, "far").reshape(half, R)
    other_left = swapped(own_left)
    left_factor = in_order(own_left, other_left, core)

    local_gram = product(left_factor, left_factor, 0, 0)
    packed = jnp.concatenate(
        [local_gram[i * BLOCK : (i + 1) * BLOCK, j * BLOCK : (j + 1) * BLOCK] for i, j in PAIRS]
    )
    share = packed.shape[0] // (2 * FAR)
    piece = lax.dynamic_slice_in_dim(packed, (core * FAR + far) * share, share, 0)
    summed = jnp.sum(from_everyone(piece, "fsdp"), axis=0)
    own_gram = from_everyone(summed, "far").reshape(-1, BLOCK)
    gram_matrix = in_order(own_gram, swapped(own_gram), core).reshape(len(PAIRS), BLOCK, BLOCK)
    high, low = inverse_factor(gram_matrix)

    partial_right = product(left_factor, blended, 0, 0).astype(bf16)
    arrived = lax.all_to_all(partial_right.reshape(8, columns, -1), "fsdp", 0, 0, tiled=True)
    right_rows = jnp.sum(arrived.astype(f32), axis=0).astype(bf16)
    raw_right = from_everyone(right_rows, "fsdp").reshape(R, -1)

    right_factor = product(high, raw_right, 1, 0) + product(low, raw_right, 1, 0)
    orthonormal = (product(left_factor, high, 1, 1) + product(left_factor, low, 1, 1)).astype(bf16)
    square_sums = jnp.sum(from_everyone(jnp.sum(right_factor * right_factor, axis=1)[None], TENSOR), axis=(0, 1))
    inverse = lax.rsqrt(square_sums + epsilon)[:, None]
    full_factor = right_factor * inverse
    own_factor = lax.dynamic_slice_in_dim(full_factor, row_group * columns, columns, 0).T
    taken = product(orthonormal, right_factor.astype(bf16), 1, 0)
    stepped = product(orthonormal, full_factor.astype(bf16), 1, 0)
    new_momentum = (blended.astype(f32) - (1.0 - decay_rate) * taken).astype(bf16)
    update = (stepped * jnp.sqrt(f32(D * FF / R))).astype(bf16)
    return (new_momentum, own_factor, update)


def solution(mesh):
    torus = Mesh(mesh.devices.reshape(mesh.shape["fsdp"], FAR, 2), ("fsdp", "far", "core"))
    return jax.shard_map(
        on_device,
        mesh=torus,
        in_specs=(P("fsdp", TENSOR), P("fsdp", TENSOR), P(TENSOR, "fsdp")),
        out_specs=(P("fsdp", TENSOR), P(TENSOR, "fsdp"), P("fsdp", TENSOR)),
        check_vma=False,
    )
```

time: 536 us -> 204 us (0.38); the launches traced: 529 us -> 204 us
  waiting for transfers between devices: 221 us -> 60.5 us
  other arithmetic: 128 us -> 4.94 us
  blocking collectives: 85.8 us -> 45.4 us
  Pallas kernels: 0 us -> 25.3 us
  starting transfers between devices: 22.7 us -> 43.5 us
  local copies, waits for them, and re-layouts: 25 us -> 6.09 us
  between operations: 17.1 us -> 0.87 us
  matrix products: 29.2 us -> 17.1 us
    psum x2 -> x0, waiting for transfers between devices: 204 us -> none  [the longest x1 107 us: on_device(): lax.psum(partial_right.astype(jnp.bfloat16), 'fsdp').astype(jnp.float32)]
    another operation x17 -> x0, other arithmetic: 120 us -> none  [the longest x14 78.6 us: on_device(): lower_factor = jnp.linalg.cholesky(gram_matrix)]
    pallas_call x0 -> x1, Pallas kernels: none -> 25.3 us  [inverse_factor(): pl.pallas_call(inverse_kernel, out_shape=[jax.ShapeDtypeStruct((R, R), bf...]
    all_to_all x2 -> x1, blocking collectives: 48.2 us -> 25.7 us  [on_device(): lax.all_to_all(partial_left.reshape(FAR, -1, R), 'far', 0, 0, tiled=True)]
    all_to_all x0 -> x1, waiting for transfers between devices: none -> 21.4 us  [on_device(): lax.all_to_all(partial_right.reshape(8, columns, -1), 'fsdp', 0, 0, tiled...]
    all_to_all x2 -> x1, blocking collectives: 37.6 us -> 19.6 us  [from_everyone(): lax.all_to_all(jnp.broadcast_to(value[None], (length, *value.shape)), axi...]
    all_to_all x2 -> x5, waiting for transfers between devices: 16.8 us -> 34.6 us  [from_everyone(): lax.all_to_all(jnp.broadcast_to(value[None], (length, *value.shape)), axi...]
    another operation x18 -> x0, local copies, waits for them, and re-layouts: 16.3 us -> none
  transfers between devices with their start and end apart: 4 -> 9, of which waited for: 4 -> 8; matrix products, arithmetic and copies ran while one was open for 2% -> 6% of each run, Pallas kernels for 0% -> 12%
where the time goes in v1:
time: 204 us
  waiting for transfers between devices  60.5 us (30%)
  blocking collectives  45.4 us (22%)
  starting transfers between devices  43.5 us (21%)
  Pallas kernels  25.3 us (12%)
  matrix products  17.1 us (8%)
  local copies, waits for them, and re-layouts  6.09 us (3%)
  other arithmetic  4.94 us (2%)
    all_to_all x5, waiting for transfers between devices, from_everyone(): lax.all_to_all(jnp.broadcast_to(value[None], (length, *value.shape)), axi...  34.6 us
    all_to_all x5, starting transfers between devices, from_everyone(): lax.all_to_all(jnp.broadcast_to(value[None], (length, *value.shape)), axi...  29.5 us
    all_to_all x1, blocking collectives, on_device(): lax.all_to_all(partial_left.reshape(FAR, -1, R), 'far', 0, 0, tiled=True)  25.7 us
    pallas_call x1, Pallas kernels, inverse_factor(): pl.pallas_call(inverse_kernel, out_shape=[jax.ShapeDtypeStruct((R, R), bf...  25.3 us
    all_to_all x1, waiting for transfers between devices, on_device(): lax.all_to_all(partial_right.reshape(8, columns, -1), 'fsdp', 0, 0, tiled...  21.4 us
    all_to_all x1, blocking collectives, from_everyone(): lax.all_to_all(jnp.broadcast_to(value[None], (length, *value.shape)), axi...  19.6 us
    dot_general x10, matrix products, product(): lax.dot_general(left, right, (((left_dim,), (right_dim,)), ((), ())), pre...  17.1 us
    ppermute x3, starting transfers between devices, swapped(): return lax.ppermute(value, 'core', [(0, 1), (1, 0)])  10.4 us
  transfers between devices with their start and end apart: 9, of which 8 were waited for; matrix products, arithmetic and copies ran while one was open for 6% of the time, Pallas kernels for 12%

profile of v1, /device:TPU:1, one launch (start us, length us, event | category | flops | bytes accessed | tf_op | source)
XLA Modules:
  0.0 203.7 jit_solution(4807380708361800685)
XLA Ops:
  0.6 0.0 copy-start
  0.6 1.1 convert_bitcast_fusion
  1.7 1.0 broadcast_in_dim.12
  2.8 11.6 %all-to-all-start = ((bf16[8,64,896]{2,1,0:T(8,128)(2,1)}), bf16[8,64,896]{2,1,0:T(8,128)(2,1)S(1)}, u32[]{:S(2)}, u32[]{:S(2)}) async-start(bf16[8,64,896]{2,1,0:T(8,128)(2,1)} %broadcast_in_dim.12), calls=%async_computation | async-start | bytes 1835008 | tf_op jit(solution)/shard_map/all_to_all | solution.py:149
  14.4 0.0 copy-done
  14.4 3.2 %add_convert_fusion = bf16[1024,896]{1,0:T(8,128)(2,1)} fusion(bf16[1024,896]{1,0:T(8,128)(2,1)S(1)} %copy-done, bf16[1024,896]{1,0:T(8,128)(2,1)} %param.3), kind=kLoop, calls=%fused_computation.2 | loop fusion | flops 3670016 | bytes 5505024 | tf_op jit(solution)/shard_map/convert_element_type | solution.py:167
  17.6 13.1 %all-to-all-done = bf16[8,64,896]{2,1,0:T(8,128)(2,1)S(1)} async-done(((bf16[8,64,896]{2,1,0:T(8,128)(2,1)}), bf16[8,64,896]{2,1,0:T(8,128)(2,1)S(1)}, u32[]{:S(2)}, u32[]{:S(2)}) %all-to-all-start) | async-done | bytes 917536 | tf_op jit(solution)/shard_map/all_to_all | solution.py:149
  30.7 2.7 %convolution_convert_fusion.1 = bf16[512,512]{1,0:T(8,128)(2,1)} fusion(bf16[512,896]{1,0:T(8,128)(2,1)S(1)} %bitcast.31, bf16[1024,896]{1,0:T(8,128)(2,1)} %add_convert_fusion, s32[]{:T(128)S(6)} %select_n.38), kind=kOutput, calls=%fused_computation.7 | convolution fusion | flops 470024192 | bytes 2359300 | tf_op jit(solution)/shard_map/dot_general | solution.py:26
  33.4 6.2 %collective-permute-start = (bf16[512,512]{1,0:T(8,128)(2,1)}, bf16[512,512]{1,0:T(8,128)(2,1)S(1)}, u32[]{:S(2)}, u32[]{:S(2)}) collective-permute-start(bf16[512,512]{1,0:T(8,128)(2,1)} %convolution_convert_fusion.1), channel_id=1, source_target_pairs={{0,1},{1,0},{2,3},{3,2},{4,5},{5,4},{6,7},{7,6},{8,9},{9,8},{10,11... | collective-permute-start | bytes 1572872 | tf_op jit(solution)/shard_map/ppermute | solution.py:153
  39.6 1.7 collective-permute-done
  41.3 0.7 add_convert_fusion.2
  42.1 25.7 %all_to_all.40 = bf16[16,32,512]{2,1,0:T(8,128)(2,1)S(1)} all-to-all(bf16[16,32,512]{2,1,0:T(8,128)(2,1)S(1)} %bitcast.34), channel_id=1, replica_groups=mesh['fsdp'=8,'far'=16,'core'=2] {'far'}, dimensions={0} | all-to-all | bytes 1048576 | tf_op jit(solution)/shard_map/all_to_all | solution.py:175
  67.8 0.1 reduce_sum.51
  67.9 19.6 %all_to_all.41 = bf16[16,32,512]{2,1,0:T(8,128)(2,1)S(1)} all-to-all(bf16[16,32,512]{2,1,0:T(8,128)(2,1)S(1)} %broadcast_in_dim.13), channel_id=1, replica_groups=mesh['fsdp'=8,'far'=16,'core'=2] {'far'}, dimensions={0} | all-to-all | bytes 1048576 | tf_op jit(solution)/shard_map/all_to_all | solution.py:149
  87.6 1.7 collective-permute-start.1
  89.3 1.5 collective-permute-done.1
  90.8 0.1 broadcast_select_fusion.1
  90.9 0.7 fusion.10
  91.7 0.0 copy-start.2
  91.9 0.7 broadcast_in_dim.14
  92.6 3.4 %all-to-all-start.3 = ((f32[8,40,128]{2,1,0:T(8,128)}), f32[8,40,128]{2,1,0:T(8,128)S(1)}, u32[]{:S(2)}, u32[]{:S(2)}) async-start(f32[8,40,128]{2,1,0:T(8,128)} %broadcast_in_dim.14), calls=%async_computation.3 | async-start | bytes 327680 | tf_op jit(solution)/shard_map/all_to_all | solution.py:149
  96.0 2.2 %convolution_convert_fusion = bf16[512,896]{1,0:T(8,128)(2,1)} fusion(bf16[1024,896]{1,0:T(8,128)(2,1)S(1)} %copy-done.2, bf16[512,512]{1,0:T(8,128)(2,1)S(1)} %get-tuple-element.8, bf16[512,512]{1,0:T(8,128)(2,1)S(1)} %get-tuple-element.7), kind=kOutput, calls=%fused_computation.6 | convolution fusion | flops 942080000 | bytes 3801088 | tf_op jit(solution)/shard_map/dot_general | solution.py:26
  98.2 7.3 %all-to-all-done.3 = f32[8,40,128]{2,1,0:T(8,128)S(1)} async-done(((f32[8,40,128]{2,1,0:T(8,128)}), f32[8,40,128]{2,1,0:T(8,128)S(1)}, u32[]{:S(2)}, u32[]{:S(2)}) %all-to-all-start.3) | async-done | bytes 163872 | tf_op jit(solution)/shard_map/all_to_all | solution.py:149
  105.4 3.6 %all-to-all-start.5 = ((bf16[8,64,896]{2,1,0:T(8,128)(2,1)}), bf16[8,64,896]{2,1,0:T(8,128)(2,1)S(1)}, u32[]{:S(2)}, u32[]{:S(2)}) async-start(bf16[8,64,896]{2,1,0:T(8,128)(2,1)} %bitcast.33), calls=%async_computation.5 | async-start | bytes 1835008 | tf_op jit(solution)/shard_map/all_to_all | solution.py:193
  109.0 21.4 %all-to-all-done.5 = bf16[8,64,896]{2,1,0:T(8,128)(2,1)S(1)} async-done(((bf16[8,64,896]{2,1,0:T(8,128)(2,1)}), bf16[8,64,896]{2,1,0:T(8,128)(2,1)S(1)}, u32[]{:S(2)}, u32[]{:S(2)}) %all-to-all-start.5) | async-done | bytes 917536 | tf_op jit(solution)/shard_map/all_to_all | solution.py:193
  130.4 0.7 broadcast_in_dim.15
  131.1 6.2 %all-to-all-start.4 = ((f32[16,40,128]{2,1,0:T(8,128)}), f32[16,40,128]{2,1,0:T(8,128)S(1)}, u32[]{:S(2)}, u32[]{:S(2)}) async-start(f32[16,40,128]{2,1,0:T(8,128)} %broadcast_in_dim.15), calls=%async_computation.4 | async-start | bytes 655360 | tf_op jit(solution)/shard_map/all_to_all | solution.py:149
  137.4 0.1 reduce_sum.53
  137.5 10.6 %all-to-all-done.4 = f32[16,40,128]{2,1,0:T(8,128)S(1)} async-done(((f32[16,40,128]{2,1,0:T(8,128)}), f32[16,40,128]{2,1,0:T(8,128)S(1)}, u32[]{:S(2)}, u32[]{:S(2)}) %all-to-all-start.4) | async-done | bytes 327712 | tf_op jit(solution)/shard_map/all_to_all | solution.py:149
  148.1 1.0 broadcast_in_dim.16
  149.2 4.4 %all-to-all-start.6 = ((bf16[8,64,896]{2,1,0:T(8,128)(2,1)}), bf16[8,64,896]{2,1,0:T(8,128)(2,1)S(1)}, u32[]{:S(2)}, u32[]{:S(2)}) async-start(bf16[8,64,896]{2,1,0:T(8,128)(2,1)} %broadcast_in_dim.16), calls=%async_computation.6 | async-start | bytes 1835008 | tf_op jit(solution)/shard_map/all_to_all | solution.py:149
  153.6 2.5 %collective-permute-start.2 = (f32[640,128]{1,0:T(8,128)S(1)}, f32[640,128]{1,0:T(8,128)S(1)}, u32[]{:S(2)}, u32[]{:S(2)}) collective-permute-start(f32[640,128]{1,0:T(8,128)S(1)} %bitcast.30), channel_id=1, source_target_pairs={{0,1},{1,0},{2,3},{3,2},{4,5},{5,4},{6,7},{7,6},{8,9},{9,8},{10,11... | collective-permute-start | bytes 983048 | tf_op jit(solution)/shard_map/ppermute | solution.py:153
  156.0 1.3 collective-permute-done.2
  157.4 25.3 %shard_map.58 = (bf16[512,512]{1,0:T(8,128)(2,1)S(1)}, bf16[512,512]{1,0:T(8,128)(2,1)S(1)}) custom-call(f32[10,128,128]{2,1,0:T(8,128)S(1)} %bitcast.26), custom_call_target="tpu_custom_call" | custom-call | flops 268435456 | bytes 2097152 | tf_op jit(solution)/shard_map/pallas_call | solution.py:132
  182.8 0.7 fusion.9
  183.5 1.7 add_convert_fusion.1
  185.2 0.0 all-to-all-done.6
  185.2 0.7 fusion.11
  185.9 0.8 multiply_reduce_fusion
  186.7 0.7 broadcast_in_dim.17
  187.4 3.9 %all-to-all-start.7 = ((f32[32,1,512]{2,1,0:T(1,128)}), f32[32,1,512]{2,1,0:T(1,128)S(1)}, u32[]{:S(2)}, u32[]{:S(2)}) async-start(f32[32,1,512]{2,1,0:T(1,128)} %broadcast_in_dim.17), calls=%async_computation.7 | async-start | bytes 131072 | tf_op jit(solution)/shard_map/all_to_all | solution.py:149
  191.3 4.3 %subtract_convert_fusion = bf16[1024,896]{1,0:T(8,128)(2,1)} fusion(bf16[1024,896]{1,0:T(8,128)(2,1)} %add_convert_fusion, bf16[1024,512]{1,0:T(8,128)(2,1)} %add_convert_fusion.1, f32[512,896]{1,0:T(8,128)S(1)} %get-tuple-element.12), kind=kOutput, calls=%fused_computation.1 | convolution fusion | flops 943652864 | bytes 6553600 | tf_op jit(solution)/shard_map/dot_general | solution.py:26
  195.6 3.6 %all-to-all-done.7 = f32[32,1,512]{2,1,0:T(1,128)S(1)} async-done(((f32[32,1,512]{2,1,0:T(1,128)}), f32[32,1,512]{2,1,0:T(1,128)S(1)}, u32[]{:S(2)}, u32[]{:S(2)}) %all-to-all-start.7) | async-done | bytes 65568 | tf_op jit(solution)/shard_map/all_to_all | solution.py:149
  199.2 0.1 reduce_sum.55
  199.3 0.2 broadcast_multiply_fusion
  199.4 1.0 copy-done.3
  200.5 2.5 %multiply_convert_fusion = bf16[1024,896]{1,0:T(8,128)(2,1)} fusion(bf16[1024,512]{1,0:T(8,128)(2,1)S(1)} %copy-done.3, f32[512,896]{1,0:T(8,128)S(1)} %broadcast_multiply_fusion), kind=kOutput, calls=%fused_computation | convolution fusion | flops 941817856 | bytes 4718592 | tf_op jit(solution)/shard_map/dot_general | solution.py:26
  203.0 0.7 dynamic-slice_bitcast_fusion
  (19 shorter events, 0.3 us)
Async XLA Ops:
  0.6 13.8 %copy-start = (bf16[1024,896]{1,0:T(8,128)(2,1)S(1)}, bf16[1024,896]{1,0:T(8,128)(2,1)}, u32[]{:S(2)}) copy-start(bf16[1024,896]{1,0:T(8,128)(2,1)} %param.4) | copy-start | bytes 5505028
  2.8 27.9 %all-to-all-start = ((bf16[8,64,896]{2,1,0:T(8,128)(2,1)}), bf16[8,64,896]{2,1,0:T(8,128)(2,1)S(1)}, u32[]{:S(2)}, u32[]{:S(2)}) async-start(bf16[8,64,896]{2,1,0:T(8,128)(2,1)} %broadcast_in_dim.12), calls=%async_computation | async-start | bytes 1835008 | tf_op jit(solution)/shard_map/all_to_all | solution.py:149
  17.6 23.7 %copy-start.1 = (bf16[1024,896]{1,0:T(8,128)(2,1)S(1)}, bf16[1024,896]{1,0:T(8,128)(2,1)}, u32[]{:S(2)}) copy-start(bf16[1024,896]{1,0:T(8,128)(2,1)} %add_convert_fusion) | copy-start | bytes 5505028
  33.4 7.9 %collective-permute-start = (bf16[512,512]{1,0:T(8,128)(2,1)}, bf16[512,512]{1,0:T(8,128)(2,1)S(1)}, u32[]{:S(2)}, u32[]{:S(2)}) collective-permute-start(bf16[512,512]{1,0:T(8,128)(2,1)} %convolution_convert_fusion.1), channel_id=1, source_target_pairs={{0,1},{1,0},{2,3},{3,2},{4,5},{5,4},{6,7},{7,6},{8,9},{9,8},{10,11... | collective-permute-start | bytes 1572872 | tf_op jit(solution)/shard_map/ppermute | solution.py:153
  87.6 3.3 %collective-permute-start.1 = (bf16[512,512]{1,0:T(8,128)(2,1)S(1)}, bf16[512,512]{1,0:T(8,128)(2,1)S(1)}, u32[]{:S(2)}, u32[]{:S(2)}) collective-permute-start(bf16[512,512]{1,0:T(8,128)(2,1)S(1)} %bitcast.29), channel_id=1, source_target_pairs={{0,1},{1,0},{2,3},{3,2},{4,5},{5,4},{6,7},{7,6},{8,9},{9,8},{10,11... | collective-permute-start | bytes 1572872 | tf_op jit(solution)/shard_map/ppermute | solution.py:153
  91.7 4.3 %copy-start.2 = (bf16[1024,896]{1,0:T(8,128)(2,1)S(1)}, bf16[1024,896]{1,0:T(8,128)(2,1)}, u32[]{:S(2)}) copy-start(bf16[1024,896]{1,0:T(8,128)(2,1)} %add_convert_fusion) | copy-start | bytes 5505028
  92.6 12.9 %all-to-all-start.3 = ((f32[8,40,128]{2,1,0:T(8,128)}), f32[8,40,128]{2,1,0:T(8,128)S(1)}, u32[]{:S(2)}, u32[]{:S(2)}) async-start(f32[8,40,128]{2,1,0:T(8,128)} %broadcast_in_dim.14), calls=%async_computation.3 | async-start | bytes 327680 | tf_op jit(solution)/shard_map/all_to_all | solution.py:149
  105.4 24.9 %all-to-all-start.5 = ((bf16[8,64,896]{2,1,0:T(8,128)(2,1)}), bf16[8,64,896]{2,1,0:T(8,128)(2,1)S(1)}, u32[]{:S(2)}, u32[]{:S(2)}) async-start(bf16[8,64,896]{2,1,0:T(8,128)(2,1)} %bitcast.33), calls=%async_computation.5 | async-start | bytes 1835008 | tf_op jit(solution)/shard_map/all_to_all | solution.py:193
  131.1 17.0 %all-to-all-start.4 = ((f32[16,40,128]{2,1,0:T(8,128)}), f32[16,40,128]{2,1,0:T(8,128)S(1)}, u32[]{:S(2)}, u32[]{:S(2)}) async-start(f32[16,40,128]{2,1,0:T(8,128)} %broadcast_in_dim.15), calls=%async_computation.4 | async-start | bytes 655360 | tf_op jit(solution)/shard_map/all_to_all | solution.py:149
  149.2 36.0 %all-to-all-start.6 = ((bf16[8,64,896]{2,1,0:T(8,128)(2,1)}), bf16[8,64,896]{2,1,0:T(8,128)(2,1)S(1)}, u32[]{:S(2)}, u32[]{:S(2)}) async-start(bf16[8,64,896]{2,1,0:T(8,128)(2,1)} %broadcast_in_dim.16), calls=%async_computation.6 | async-start | bytes 1835008 | tf_op jit(solution)/shard_map/all_to_all | solution.py:149
  153.6 3.7 %collective-permute-start.2 = (f32[640,128]{1,0:T(8,128)S(1)}, f32[640,128]{1,0:T(8,128)S(1)}, u32[]{:S(2)}, u32[]{:S(2)}) collective-permute-start(f32[640,128]{1,0:T(8,128)S(1)} %bitcast.30), channel_id=1, source_target_pairs={{0,1},{1,0},{2,3},{3,2},{4,5},{5,4},{6,7},{7,6},{8,9},{9,8},{10,11... | collective-permute-start | bytes 983048 | tf_op jit(solution)/shard_map/ppermute | solution.py:153
  187.4 11.8 %all-to-all-start.7 = ((f32[32,1,512]{2,1,0:T(1,128)}), f32[32,1,512]{2,1,0:T(1,128)S(1)}, u32[]{:S(2)}, u32[]{:S(2)}) async-start(f32[32,1,512]{2,1,0:T(1,128)} %broadcast_in_dim.17), calls=%async_computation.7 | async-start | bytes 131072 | tf_op jit(solution)/shard_map/all_to_all | solution.py:149
  199.2 1.2 copy-start.3
